TPU v7x, 32 devices: a whole 2x2x4 slice. The times are simulated.
32 devices in a mesh: rep: 8 (over y, x, core), fsdp: 4 (over z).
Axes of the slice: x: 2, y: 2, z: 4, core: 2. Of those that a mesh axis runs over, the one named last changes fastest.
Arguments:
- tokens: bfloat16 [4096, 4096], P('rep', 'fsdp'), may hold values from -6 to 6
- gate_weight: bfloat16 [4096, 7168], P('rep', 'fsdp'), may hold values from -0.09375 to 0.09375
- up_act: bfloat16 [4096, 7168], P('rep', 'fsdp'), may hold values from -6 to 6
- cotangent: bfloat16 [4096, 7168], P('rep', 'fsdp'), may hold values from -0.099609375 to 0.099609375
Outputs:
- grad_sum: bfloat16 [4096, 7168], P('rep', 'fsdp')
- curvature: float32 [7168], P('fsdp')
- spread: float32 [7168], P('fsdp')
All inputs are finite; a program needn't handle non-finite values.
Results may differ from a plain program's by a relative error of at most 0.024.
Values may be sent and summed in bfloat16 or wider, within the bound.
A program may use at most 128 MiB of HBM per device.

v0:
```python
import jax
import jax.numpy as jnp
from jax import lax
from jax.sharding import PartitionSpec as P


def shards(tokens, gate_weight, up_act, cotangent):
    features_all = lax.all_gather(tokens, "fsdp", axis=1, tiled=True)
    replicas = lax.axis_size("rep")

    def add_rows(block_rows):
        return jnp.dot(features_all, block_rows, preferred_element_type=jnp.float32)

    gate_pre = add_rows(lax.all_gather(gate_weight, "rep", axis=0, tiled=True))
    sigmoid_gate = jax.nn.sigmoid(gate_pre)
    deriv_one = sigmoid_gate * (1.0 + gate_pre * (1.0 - sigmoid_gate))
    deriv_two = sigmoid_gate * (1.0 - sigmoid_gate) * (2.0 + gate_pre * (1.0 - 2.0 * sigmoid_gate))
    weighted = cotangent.astype(jnp.float32) * up_act.astype(jnp.float32)
    token_coeff = (weighted * deriv_one).astype(jnp.bfloat16)
    bend_weight = weighted * deriv_two
    rep_grad = lax.dot_general(
        features_all, token_coeff, (((0,), (0,)), ((), ())), preferred_element_type=jnp.float32
    ).astype(jnp.bfloat16)
    own_proj = jnp.dot(features_all, rep_grad, preferred_element_type=jnp.float32)
    grad_shard = lax.psum_scatter(
        rep_grad.astype(jnp.float32).astype(jnp.bfloat16), "rep", scatter_dimension=0, tiled=True
    )
    mean_proj = add_rows(lax.all_gather(grad_shard, "rep", axis=0, tiled=True)) / replicas
    deviate = own_proj - mean_proj
    curv_part = jnp.sum(bend_weight * mean_proj * mean_proj, axis=0)
    spread_part = jnp.sum(bend_weight * deviate * deviate, axis=0)
    curvature, spread_total = lax.psum((curv_part, spread_part), "rep")
    return (grad_shard, curvature, spread_total / (replicas - 1))


def solution(mesh):
    placed = (P("rep", "fsdp"), P("rep", "fsdp"), P("rep", "fsdp"), P("rep", "fsdp"))
    return jax.shard_map(
        shards,
        mesh=mesh,
        in_specs=placed,
        out_specs=(P("rep", "fsdp"), P("fsdp"), P("fsdp")),
        check_vma=False,
    )
```

profile of v0, /device:TPU:0, one launch (start us, length us, event | category | flops | bytes accessed | tf_op | source)
XLA Modules:
  0.0 455.3 jit_solution(8435540799089013819)
XLA Ops:
  7.2 0.0 all-gather.4.cloned.1.call-start
  7.2 0.7 all-gather.4.cloned.1.call-update
  7.9 0.0 all-gather.6.cloned.1.call-start
  7.9 0.7 all-gather.6.cloned.1.call-update
  8.6 0.0 copy-start.2
  8.7 0.0 reduce-scatter.2.cloned.1.call-start
  8.7 84.3 %all-gather.4.cloned.1.call-done = bf16[512,4096]{1,0:T(8,128)(2,1)} async-done(((bf16[512,1024]{1,0:T(8,128)(2,1)}), bf16[512,4096]{1,0:T(8,128)(2,1)}) %all-gather.4.cloned.1.call-update) | async-done | bytes 4194320 | tf_op jit(solution)/shard_map/all_gather | solution.py:8
  93.0 81.3 %all-gather.6.cloned.1.call-done = bf16[4096,1792]{1,0:T(8,128)(2,1)} async-done(((bf16[512,1792]{1,0:T(8,128)(2,1)}), bf16[4096,1792]{1,0:T(8,128)(2,1)}) %all-gather.6.cloned.1.call-update) | async-done | bytes 14680080 | tf_op jit(solution)/shard_map/all_gather | solution.py:14
  174.3 16.7 %fusion.11 = f32[512,1792]{1,0:T(8,128)} fusion(bf16[512,4096]{1,0:T(8,128)(2,1)} %all-gather.4.cloned.1.call-done, bf16[4096,1792]{1,0:T(8,128)(2,1)} %all-gather.6.cloned.1.call-done), kind=kOutput, calls=%fused_computation.20 | convolution fusion | flops 7516192768 | bytes 22544384 | tf_op jit(solution)/shard_map/dot_general | solution.py:12
  191.0 0.0 copy-done.2
  191.0 0.0 copy-done
  191.0 0.0 copy-done.3
  191.0 15.3 %convolution_convert_fusion = bf16[1792,4096]{1,0:T(8,128)(2,1)} fusion(bf16[512,4096]{1,0:T(8,128)(2,1)S(1)} %copy-done, f32[512,1792]{1,0:T(8,128)} %fusion.11, bf16[512,1792]{1,0:T(8,128)(2,1)S(1)} %copy-done.2, bf16[512,1792]{1,0:T(8,128)(2,1)S(1)} %copy-done.3), kind=kOutput, calls=%fused_computation | convolution fusion | flops 7534542848 | bytes 26214400 | tf_op jit(solution)/shard_map/dot_general | solution.py:21
  206.3 0.0 reduce-scatter.2.cloned.1.call-update
  206.4 0.2 all-gather.8.cloned.1.call-start
  206.6 102.2 %reduce-scatter.2.cloned.1.call-done = bf16[512,1792]{0,1:T(8,128)(2,1)} async-done(((bf16[4096,1792]{0,1:T(8,128)(2,1)}), bf16[512,1792]{0,1:T(8,128)(2,1)}) %reduce-scatter.2.cloned.1.call-update) | async-done | bytes 1835024 | tf_op jit(solution)/shard_map/reduce_scatter | solution.py:25
  308.8 0.0 all-gather.8.cloned.1.call-update
  308.8 3.8 copy.7
  312.6 81.6 %all-gather.8.cloned.1.call-done = bf16[4096,1792]{0,1:T(8,128)(2,1)} async-done(((bf16[512,1792]{0,1:T(8,128)(2,1)}), bf16[4096,1792]{0,1:T(8,128)(2,1)}) %all-gather.8.cloned.1.call-update) | async-done | bytes 14680080 | tf_op jit(solution)/shard_map/all_gather | solution.py:28
  394.2 16.5 %fusion.6 = (f32[1792]{0:T(1024)S(1)}, f32[1792,512]{0,1:T(8,128)S(1)}) fusion(f32[512,1792]{1,0:T(8,128)} %fusion.11, bf16[512,1792]{1,0:T(8,128)(2,1)S(1)} %copy-done.2, bf16[512,1792]{1,0:T(8,128)(2,1)} %param.7, bf16[4096,1792]{0,1:T(8,128)(2,1)} %all-gather.8.cloned.1.call-done, bf16[512,4096]{1,0:T(8,128)(2,1)} %all-gather.4.cloned.1.call-done), kind=kOutput, calls=%fused_computation.11 | convolution fusion | flops 7532705792 | bytes 29891584 | tf_op jit(solution)/shard_map/dot_general | solution.py:12
  410.8 0.0 copy-done.1
  410.8 13.8 %fusion.7 = f32[1792]{0:T(1024)S(1)} fusion(f32[1792,512]{0,1:T(8,128)S(1)} %get-tuple-element.9, bf16[1792,4096]{1,0:T(8,128)(2,1)} %convolution_convert_fusion, bf16[512,4096]{1,0:T(8,128)(2,1)S(1)} %copy-done.1, f32[512,1792]{1,0:T(8,128)S(1)} %copy-done.5, bf16[512,1792]{1,0:T(8,128)(2,1)S(1)} %copy-done.2, bf16[512,1792]{1,0:T(8,128)(2,1)S(1)} %copy-done.4), kind=kOutput, calls=%fused_computation.12 | convolution fusion | flops 7532705792 | bytes 29891584 | tf_op jit(solution)/shard_map/dot_general | solution.py:24
  424.7 23.5 %all-reduce = (f32[1792]{0:T(1024)}, f32[1792]{0:T(1024)S(1)}) all-reduce(f32[1792]{0:T(1024)S(1)} %get-tuple-element.8, f32[1792]{0:T(1024)S(1)} %fusion.7), channel_id=1, replica_groups=mesh['rep'=8,'fsdp'=4] {'rep'}, use_global_device_ids=true, to_apply=%region_2.0 | all-reduce | flops 3584 | bytes 28672 | tf_op jit(solution)/shard_map/psum | solution.py:32
  448.1 0.6 broadcast_multiply_fusion
  (7 shorter events, 0.0 us)
Async XLA Ops:
  7.2 85.9 %all-gather.4.cloned.1.call-start = ((), (), s32[]{:S(2)}) async-start(), calls=%async_computation.1 | async-start | bytes 5242880 | tf_op jit(solution)/shard_map/all_gather | solution.py:8
  7.9 166.4 %all-gather.6.cloned.1.call-start = ((), (), s32[]{:S(2)}) async-start(), calls=%async_computation.2 | async-start | bytes 16515072 | tf_op jit(solution)/shard_map/all_gather | solution.py:14
  8.6 182.4 %copy-start.2 = (bf16[512,1792]{1,0:T(8,128)(2,1)S(1)}, bf16[512,1792]{1,0:T(8,128)(2,1)}, u32[]{:S(2)}) copy-start(bf16[512,1792]{1,0:T(8,128)(2,1)} %param.6) | copy-start | bytes 5505028
  8.7 300.1 %reduce-scatter.2.cloned.1.call-start = ((), (), s32[]{:S(2)}) async-start(), calls=%async_computation.3 | async-start | bytes 16515072 | tf_op jit(solution)/shard_map/reduce_scatter | solution.py:25
  174.3 16.7 %copy-start = (bf16[512,4096]{1,0:T(8,128)(2,1)S(1)}, bf16[512,4096]{1,0:T(8,128)(2,1)}, u32[]{:S(2)}) copy-start(bf16[512,4096]{1,0:T(8,128)(2,1)} %all-gather.4.cloned.1.call-done) | copy-start | bytes 12582916
  174.3 16.7 %copy-start.3 = (bf16[512,1792]{1,0:T(8,128)(2,1)S(1)}, bf16[512,1792]{1,0:T(8,128)(2,1)}, u32[]{:S(2)}) copy-start(bf16[512,1792]{1,0:T(8,128)(2,1)} %param.7) | copy-start | bytes 5505028
  206.4 187.9 %all-gather.8.cloned.1.call-start = ((), (), s32[]{:S(2)}) async-start(), calls=%async_computation.4 | async-start | bytes 16515072 | tf_op jit(solution)/shard_map/all_gather | solution.py:28
  394.2 16.5 %copy-start.1 = (bf16[512,4096]{1,0:T(8,128)(2,1)S(1)}, bf16[512,4096]{1,0:T(8,128)(2,1)}, u32[]{:S(2)}) copy-start(bf16[512,4096]{1,0:T(8,128)(2,1)} %all-gather.4.cloned.1.call-done) | copy-start | bytes 12582916
  394.2 16.6 %copy-start.4 = (bf16[512,1792]{1,0:T(8,128)(2,1)S(1)}, bf16[512,1792]{1,0:T(8,128)(2,1)}, u32[]{:S(2)}) copy-start(bf16[512,1792]{1,0:T(8,128)(2,1)} %param.7) | copy-start | bytes 5505028
  394.2 16.6 %copy-start.5 = (f32[512,1792]{1,0:T(8,128)S(1)}, f32[512,1792]{1,0:T(8,128)}, u32[]{:S(2)}) copy-start(f32[512,1792]{1,0:T(8,128)} %fusion.11) | copy-start | bytes 11010052
Sparse Core Ops, SparseCore 0:
  9.5 83.4 all-gather.3
  94.9 79.3 all-gather.5
  206.5 102.2 reduce-scatter.1
  310.5 83.7 all-gather.7
where the time goes:
time: 456 us; the launch traced here: 455 us
  waiting for transfers between devices  351 us (77%)
  matrix products  62.4 us (14%)
  blocking collectives  23.5 us (5%)
  between operations  13.8 us (3%)
    reduce_scatter x1, waiting for transfers between devices, shards(): lax.psum_scatter(rep_grad.astype(jnp.float32).astype(jnp.bfloat16), 'rep'...  102 us
    all_gather x1, waiting for transfers between devices, shards(): features_all = lax.all_gather(tokens, 'fsdp', axis=1, tiled=True)  84.3 us
    all_gather x1, waiting for transfers between devices, shards(): lax.all_gather(grad_shard, 'rep', axis=0, tiled=True)  81.6 us
    all_gather x1, waiting for transfers between devices, shards(): gate_pre = add_rows(lax.all_gather(gate_weight, 'rep', axis=0, tiled=True))  81.3 us
    dot_general x2, matrix products, add_rows(): return jnp.dot(features_all, block_rows, preferred_element_type=jnp.float32)  33.2 us
    psum x1, blocking collectives, shards(): curvature, spread_total = lax.psum((curv_part, spread_part), 'rep')  23.5 us
    dot_general x1, matrix products, shards(): lax.dot_general(features_all, token_coeff, (((0,), (0,)), ((), ())), pref...  15.3 us
    dot_general x1, matrix products, shards(): jnp.dot(features_all, rep_grad, preferred_element_type=jnp.float32)  13.8 us
  transfers between devices with their start and end apart: 4, of which 4 were waited for; matrix products, arithmetic and copies ran while one was open for 1% of the time, Pallas kernels for 0%

commit v1 on v0

--- a/solution.py
+++ b/solution.py
@@ -5,7 +5,7 @@
 
 
 def shards(tokens, gate_weight, up_act, cotangent):
-    features_all = lax.all_gather(tokens, "fsdp", axis=1, tiled=True)
+    features_all = jnp.concatenate(lax.all_gather(tokens, "fsdp"), axis=1)
     replicas = lax.axis_size("rep")
 
     def add_rows(block_rows):

time: 456 us -> 461 us (1.011)
  local copies, waits for them, and re-layouts: 3.83 us -> 10 us
  waiting for transfers between devices: 351 us -> 345 us
  matrix products: 62.4 us -> 67.6 us
    all_gather x1, waiting for transfers between devices: 81.3 us -> 75.1 us  [shards(): gate_pre = add_rows(lax.all_gather(gate_weight, 'rep', axis=0, tiled=True))]
    reshape x0 -> x1, local copies, waits for them, and re-layouts: none -> 6.21 us  [shards(): features_all = jnp.concatenate(lax.all_gather(tokens, 'fsdp'), axis=1)]
  transfers between devices with their start and end apart: 4 -> 4, of which waited for: 4 -> 4; matrix products, arithmetic and copies ran while one was open for 1% -> 2% of each run, Pallas kernels for 0% -> 0%
where the time goes in v1:
time: 461 us; the launch traced here: 460 us
  waiting for transfers between devices  345 us (75%)
  matrix products  67.6 us (15%)
  blocking collectives  23.5 us (5%)
  between operations  13.8 us (3%)
  local copies, waits for them, and re-layouts  10 us (2%)
    reduce_scatter x1, waiting for transfers between devices, shards(): lax.psum_scatter(rep_grad.astype(jnp.float32).astype(jnp.bfloat16), 'rep'...  102 us
    all_gather x1, waiting for transfers between devices, shards(): features_all = jnp.concatenate(lax.all_gather(tokens, 'fsdp'), axis=1)  84.3 us
    all_gather x1, waiting for transfers between devices, shards(): lax.all_gather(grad_shard, 'rep', axis=0, tiled=True)  81.7 us
    all_gather x1, waiting for transfers between devices, shards(): gate_pre = add_rows(lax.all_gather(gate_weight, 'rep', axis=0, tiled=True))  75.1 us
    dot_general x2, matrix products, add_rows(): return jnp.dot(features_all, block_rows, preferred_element_type=jnp.float32)  34.5 us
    psum x1, blocking collectives, shards(): curvature, spread_total = lax.psum((curv_part, spread_part), 'rep')  23.5 us
    dot_general x1, matrix products, shards(): jnp.dot(features_all, rep_grad, preferred_element_type=jnp.float32)  17 us
    dot_general x1, matrix products, shards(): lax.dot_general(features_all, token_coeff, (((0,), (0,)), ((), ())), pref...  16.2 us
  transfers between devices with their start and end apart: 4, of which 4 were waited for; matrix products, arithmetic and copies ran while one was open for 2% of the time, Pallas kernels for 0%

profile of v1, /device:TPU:0, one launch (start us, length us, event | category | flops | bytes accessed | tf_op | source)
XLA Modules:
  0.0 460.4 jit_solution(15194610680115751713)
XLA Ops:
  7.2 0.0 all-gather.9.cloned.1.call-start
  7.2 0.7 all-gather.9.cloned.1.call-update
  7.9 0.0 all-gather.5.cloned.1.call-start
  7.9 0.7 all-gather.5.cloned.1.call-update
  8.6 0.0 reduce-scatter.2.cloned.1.call-start
  8.7 84.3 %all-gather.9.cloned.1.call-done = bf16[2048,1024]{1,0:T(8,128)(2,1)} async-done(((bf16[512,1024]{1,0:T(8,128)(2,1)}), bf16[2048,1024]{1,0:T(8,128)(2,1)}) %all-gather.9.cloned.1.call-update) | async-done | bytes 4194320 | tf_op jit(solution)/shard_map/all_gather | solution.py:8
  93.0 6.2 %copy.9 = bf16[512,4,1024]{0,2,1:T(8,128)(2,1)} copy(bf16[512,4,1024]{2,0,1:T(8,128)(2,1)} %bitcast.24) | data formatting | bytes 8388608 | tf_op jit(solution)/shard_map/reshape | solution.py:8
  99.2 75.1 %all-gather.5.cloned.1.call-done = bf16[4096,1792]{1,0:T(8,128)(2,1)} async-done(((bf16[512,1792]{1,0:T(8,128)(2,1)}), bf16[4096,1792]{1,0:T(8,128)(2,1)}) %all-gather.5.cloned.1.call-update) | async-done | bytes 14680080 | tf_op jit(solution)/shard_map/all_gather | solution.py:14
  174.3 0.0 copy-start
  174.3 0.0 copy-start.1
  174.3 16.6 %fusion.11 = f32[512,1792]{1,0:T(8,128)} fusion(bf16[512,4096]{0,1:T(8,128)(2,1)} %bitcast.20, bf16[4096,1792]{1,0:T(8,128)(2,1)} %all-gather.5.cloned.1.call-done), kind=kOutput, calls=%fused_computation.20 | convolution fusion | flops 7516192768 | bytes 22544384 | tf_op jit(solution)/shard_map/dot_general | solution.py:12
  191.0 0.0 copy-done
  191.0 0.0 copy-done.1
  191.0 16.2 %convolution_convert_fusion = bf16[1792,4096]{1,0:T(8,128)(2,1)} fusion(bf16[512,4096]{0,1:T(8,128)(2,1)S(1)} %bitcast.23, f32[512,1792]{1,0:T(8,128)} %fusion.11, bf16[512,1792]{1,0:T(8,128)(2,1)S(1)} %copy-done.1, bf16[512,1792]{1,0:T(8,128)(2,1)} %param.7), kind=kOutput, calls=%fused_computation | convolution fusion | flops 7534542848 | bytes 26214400 | tf_op jit(solution)/shard_map/dot_general | solution.py:21
  207.2 0.0 reduce-scatter.2.cloned.1.call-update
  207.2 0.2 all-gather.7.cloned.1.call-start
  207.4 102.1 %reduce-scatter.2.cloned.1.call-done = bf16[512,1792]{0,1:T(8,128)(2,1)} async-done(((bf16[4096,1792]{0,1:T(8,128)(2,1)}), bf16[512,1792]{0,1:T(8,128)(2,1)}) %reduce-scatter.2.cloned.1.call-update) | async-done | bytes 1835024 | tf_op jit(solution)/shard_map/reduce_scatter | solution.py:25
  309.5 0.0 all-gather.7.cloned.1.call-update
  309.6 3.8 copy.10
  313.4 81.7 %all-gather.7.cloned.1.call-done = bf16[4096,1792]{0,1:T(8,128)(2,1)} async-done(((bf16[512,1792]{0,1:T(8,128)(2,1)}), bf16[4096,1792]{0,1:T(8,128)(2,1)}) %all-gather.7.cloned.1.call-update) | async-done | bytes 14680080 | tf_op jit(solution)/shard_map/all_gather | solution.py:28
  395.0 17.8 %fusion.6 = (f32[1792]{0:T(1024)S(1)}, f32[1792,512]{0,1:T(8,128)}) fusion(f32[512,1792]{1,0:T(8,128)} %fusion.11, bf16[512,1792]{1,0:T(8,128)(2,1)S(1)} %copy-done.1, bf16[512,1792]{1,0:T(8,128)(2,1)} %param.7, bf16[4096,1792]{0,1:T(8,128)(2,1)} %all-gather.7.cloned.1.call-done, bf16[512,4096]{0,1:T(8,128)(2,1)} %bitcast.21), kind=kOutput, calls=%fused_computation.11 | convolution fusion | flops 7532705792 | bytes 29891584 | tf_op jit(solution)/shard_map/dot_general | solution.py:12
  412.8 17.0 %fusion.7 = f32[1792]{0:T(1024)S(1)} fusion(f32[1792,512]{0,1:T(8,128)} %get-tuple-element.15, bf16[1792,4096]{1,0:T(8,128)(2,1)} %convolution_convert_fusion, bf16[512,4096]{0,1:T(8,128)(2,1)} %bitcast.22, f32[512,1792]{1,0:T(8,128)} %fusion.11, bf16[512,1792]{1,0:T(8,128)(2,1)S(1)} %copy-done.1, bf16[512,1792]{1,0:T(8,128)(2,1)} %param.7), kind=kOutput, calls=%fused_computation.12 | convolution fusion | flops 7532705792 | bytes 29891584 | tf_op jit(solution)/shard_map/dot_general | solution.py:24
  429.8 23.5 %all-reduce = (f32[1792]{0:T(1024)}, f32[1792]{0:T(1024)S(1)}) all-reduce(f32[1792]{0:T(1024)S(1)} %get-tuple-element.14, f32[1792]{0:T(1024)S(1)} %fusion.7), channel_id=1, replica_groups=mesh['rep'=8,'fsdp'=4] {'rep'}, use_global_device_ids=true, to_apply=%region_2.0 | all-reduce | flops 3584 | bytes 28672 | tf_op jit(solution)/shard_map/psum | solution.py:32
  453.3 0.6 broadcast_multiply_fusion
Async XLA Ops:
  7.2 85.9 %all-gather.9.cloned.1.call-start = ((), (), s32[]{:S(2)}) async-start(), calls=%async_computation.4 | async-start | bytes 5242880 | tf_op jit(solution)/shard_map/all_gather | solution.py:8
  7.9 166.4 %all-gather.5.cloned.1.call-start = ((), (), s32[]{:S(2)}) async-start(), calls=%async_computation.1 | async-start | bytes 16515072 | tf_op jit(solution)/shard_map/all_gather | solution.py:14
  8.6 300.9 %reduce-scatter.2.cloned.1.call-start = ((), (), s32[]{:S(2)}) async-start(), calls=%async_computation.2 | async-start | bytes 16515072 | tf_op jit(solution)/shard_map/reduce_scatter | solution.py:25
  174.3 16.6 %copy-start = (bf16[512,4,1024]{0,2,1:T(8,128)(2,1)S(1)}, bf16[512,4,1024]{0,2,1:T(8,128)(2,1)}, u32[]{:S(2)}) copy-start(bf16[512,4,1024]{0,2,1:T(8,128)(2,1)} %copy.9) | copy-start | bytes 12582916
  174.3 16.6 %copy-start.1 = (bf16[512,1792]{1,0:T(8,128)(2,1)S(1)}, bf16[512,1792]{1,0:T(8,128)(2,1)}, u32[]{:S(2)}) copy-start(bf16[512,1792]{1,0:T(8,128)(2,1)} %param.6) | copy-start | bytes 5505028
  207.2 187.8 %all-gather.7.cloned.1.call-start = ((), (), s32[]{:S(2)}) async-start(), calls=%async_computation.3 | async-start | bytes 16515072 | tf_op jit(solution)/shard_map/all_gather | solution.py:28
Sparse Core Ops, SparseCore 0:
  9.5 83.4 all-gather.8
  94.9 79.3 all-gather.4
  207.3 102.1 reduce-scatter.1
  311.3 83.7 all-gather.6
